TPU v7x, 512 devices: a whole 4x4x16 slice. The times are simulated.
512 devices in a mesh: gx: 8 (over z_lo), gy: 4 (over z_hi, core), gz: 16 (over y, x).
Axes of the slice: x: 4, y: 4, z: 16 (z_hi: 2, z_lo: 8; z = z_hi * 8 + z_lo), core: 2. Of those that a mesh axis runs over, the one named last changes fastest.
Arguments:
- probe_vectors: float32 [32, 16, 32, 2048], P(None, 'gx', 'gy', 'gz'), may hold values from -6 to 6
- layer_ids: int32 [16, 32, 2048], P('gx', 'gy', 'gz'), may hold values from 0 to 15
- layer_kappa: float32 [16], replicated, may hold values from 0.1 to 10
- slot_order: int32 [32, 16], replicated, may hold values from 0 to 511, as said below
Outputs:
- factored: float32 [16384, 16384], P(('gx', 'gy'), 'gz')
Inputs may be any that keep to these rules, and one draw needn't show every extreme that they name: `slot_order`: the entries are an ordering of 0 to 511, and in each column the entries divided by 16, rounded down, are an ordering of 0 to 31.
All inputs are finite; a program needn't handle non-finite values.
Results may differ from a plain program's by a relative error of at most 0.00013.
Values sent between devices are 32-bit elements; how exact they have to be, the bound alone decides.
No kernel may reach another device: no remote copies, remote signals or barrier semaphores. Data moves between devices by JAX's collectives and lax.ppermute only.
A program may use at most 128 MiB of HBM per device.

v0:
```python
import math
import jax
import jax.numpy as jnp
from jax import lax
from jax.sharding import PartitionSpec as P

PASSES = 4
PANEL = 256
NPAN = 2
upper_edge = 120.0
lower_edge = 24.0
coarse_shift = 1.0


def with_halo(block, sides, width):
    for axis, dim in sides:
        count = lax.axis_size(axis)
        forward = [(i, i + 1) for i in range(count - 1)]
        backward = [(target, source) for source, target in forward]
        low = lax.ppermute(
            lax.slice_in_dim(block, block.shape[dim] - width, None, axis=dim), axis, forward
        )
        high = lax.ppermute(lax.slice_in_dim(block, 0, width, axis=dim), axis, backward)
        block = jnp.concatenate([low, block, high], axis=dim)
    return block


def from_root(value, axis, source):
    kept = jnp.where(lax.axis_index(axis) == source, value, 0).astype(value.dtype)
    return lax.psum(kept, axis)


def cheb_factors(step_index):
    center = (upper_edge + lower_edge) / (upper_edge - lower_edge)
    growth = math.log(center + math.sqrt(center * center - 1.0))

    def chebval(degree):
        expo = math.exp(degree * growth)
        return 0.5 * (expo + 1.0 / expo)

    if step_index == 0:
        return (1.0 / chebval(1), 0.0)
    return (
        2.0 * chebval(step_index) / chebval(step_index + 1),
        chebval(step_index - 1) / chebval(step_index + 1),
    )


def face_weights(kappa_pad):
    center = kappa_pad[1:-1, 1:-1, 1:-1]
    x_plus = 0.5 * (center + kappa_pad[2:, 1:-1, 1:-1])
    x_minus = 0.5 * (center + kappa_pad[:-2, 1:-1, 1:-1])
    y_plus = 0.5 * (center + kappa_pad[1:-1, 2:, 1:-1])
    y_minus = 0.5 * (center + kappa_pad[1:-1, :-2, 1:-1])
    z_plus = 0.5 * (center + kappa_pad[1:-1, 1:-1, 2:])
    z_minus = 0.5 * (center + kappa_pad[1:-1, 1:-1, :-2])
    diagonal = x_plus + x_minus + y_plus + y_minus + z_plus + z_minus
    return ((x_plus, x_minus, y_plus, y_minus, z_plus, z_minus), diagonal)


def apply_operator(field_pad, weights, diagonal):
    x_plus, x_minus, y_plus, y_minus, z_plus, z_minus = weights
    interior = field_pad[..., 1:-1, 1:-1, 1:-1]
    beside = x_plus * field_pad[..., 2:, 1:-1, 1:-1] + x_minus * field_pad[..., :-2, 1:-1, 1:-1]
    beside = (
        beside + y_plus * field_pad[..., 1:-1, 2:, 1:-1] + y_minus * field_pad[..., 1:-1, :-2, 1:-1]
    )
    beside = (
        beside + z_plus * field_pad[..., 1:-1, 1:-1, 2:] + z_minus * field_pad[..., 1:-1, 1:-1, :-2]
    )
    return diagonal * interior - beside


def cheb_update(current, previous, applied, step_index):
    factor_one, factor_two = cheb_factors(step_index)
    shifted = (upper_edge + lower_edge) / (upper_edge - lower_edge) * current - 2.0 / (
        upper_edge - lower_edge
    ) * applied
    return factor_one * shifted - factor_two * previous


def face_block(own_face, weight_face, ghost_face, scaling):
    return -scaling * jnp.einsum(
        "kab,ab,lab->kl", own_face, weight_face, ghost_face, precision=lax.Precision.HIGHEST
    )


def table_lookup(table, row_wanted, col_wanted):
    row_ids = jnp.arange(table.shape[0], dtype=jnp.int32)
    col_ids = jnp.arange(table.shape[1], dtype=jnp.int32)
    hit = (row_wanted[..., None, None] == row_ids[:, None]) & (
        col_wanted[..., None, None] == col_ids[None, :]
    )
    return jnp.sum(jnp.where(hit, table, 0), axis=(-2, -1))


def on_device(probe_vectors, layer_ids, layer_kappa, slot_order):
    highest = lax.Precision.HIGHEST
    grid_x = lax.axis_size("gx")
    grid_y = lax.axis_size("gy")
    grid_z = lax.axis_size("gz")
    index_x = lax.axis_index("gx")
    index_y = lax.axis_index("gy")
    index_z = lax.axis_index("gz")
    vectors, extent_x, extent_y, extent_z = probe_vectors.shape
    layers = layer_kappa.shape[0]
    choose = layer_ids[None] == jnp.arange(layers, dtype=jnp.int32)[:, None, None, None]
    conductivity = jnp.sum(jnp.where(choose, layer_kappa[:, None, None, None], 0.0), axis=0)
    kappa_pad = with_halo(conductivity, (("gx", 0), ("gy", 1), ("gz", 2)), 1)
    weights, diagonal = face_weights(kappa_pad)
    current = probe_vectors
    previous = jnp.zeros_like(probe_vectors)
    for step_index in range(PASSES):
        padded = with_halo(current, (("gx", 1), ("gy", 2), ("gz", 3)), 1)
        applied = apply_operator(padded, weights, diagonal)
        current, previous = (cheb_update(current, previous, applied, step_index), current)
    ghosts = with_halo(current, (("gx", 1), ("gy", 2), ("gz", 3)), 1)
    local_image = apply_operator(
        jnp.pad(current, ((0, 0), (1, 1), (1, 1), (1, 1))), weights, diagonal
    )
    cell_count = extent_x * extent_y * extent_z
    scaling = 1.0 / math.sqrt(cell_count)
    flattened = current.reshape(vectors, cell_count)
    own_block = scaling * jnp.dot(
        flattened, local_image.reshape(vectors, cell_count).T, precision=highest
    )
    own_block = own_block + coarse_shift * jnp.eye(vectors, dtype=jnp.float32)
    x_plus, x_minus, y_plus, y_minus, z_plus, z_minus = weights
    blocks = jnp.stack(
        [
            own_block,
            face_block(current[:, 0], x_minus[0], ghosts[:, 0, 1:-1, 1:-1], scaling),
            face_block(current[:, -1], x_plus[-1], ghosts[:, -1, 1:-1, 1:-1], scaling),
            face_block(current[:, :, 0], y_minus[:, 0], ghosts[:, 1:-1, 0, 1:-1], scaling),
            face_block(current[:, :, -1], y_plus[:, -1], ghosts[:, 1:-1, -1, 1:-1], scaling),
            face_block(current[:, :, :, 0], z_minus[:, :, 0], ghosts[:, 1:-1, 1:-1, 0], scaling),
            face_block(current[:, :, :, -1], z_plus[:, :, -1], ghosts[:, 1:-1, 1:-1, -1], scaling),
        ]
    )
    rows_total = grid_x * grid_y
    row_index = index_x * grid_y + index_y
    row_ids = jnp.arange(rows_total, dtype=jnp.int32)
    group_of = slot_order // grid_z
    column_groups = lax.dynamic_index_in_dim(group_of, index_z, 1, keepdims=False)
    owner_source = jnp.sum(jnp.where(column_groups == row_index, row_ids, 0))
    piece = lax.all_gather(blocks[None], ("gx", "gy"), axis=0, tiled=True)
    anchor = jnp.arange(piece.shape[0], dtype=jnp.int32)
    wanted = (anchor == owner_source)[:, None, None, None]
    owned = jnp.sum(jnp.where(wanted, piece, 0.0), axis=0)
    sources = jnp.arange(grid_z, dtype=jnp.int32)
    source_rows = jnp.sum(jnp.where(group_of == row_index, row_ids[:, None], 0), axis=0)
    source_x = source_rows // grid_y
    source_y = source_rows % grid_y
    neighbour_rows = jnp.stack(
        [
            source_rows,
            source_rows - grid_y,
            source_rows + grid_y,
            source_rows - 1,
            source_rows + 1,
            source_rows,
            source_rows,
        ],
        axis=1,
    )
    neighbour_cols = jnp.stack(
        [sources, sources, sources, sources, sources, sources - 1, sources + 1], axis=1
    )
    always = jnp.ones((grid_z,), bool)
    usable = jnp.stack(
        [
            always,
            source_x > 0,
            source_x < grid_x - 1,
            source_y > 0,
            source_y < grid_y - 1,
            sources > 0,
            sources < grid_z - 1,
        ],
        axis=1,
    )
    targets = table_lookup(slot_order, neighbour_rows, neighbour_cols)
    own_slots = table_lookup(slot_order, source_rows, sources) - row_index * grid_z
    local_cols = targets - index_z * rows_total
    usable = usable & (local_cols >= 0) & (local_cols < rows_total)
    col_flat = jnp.where(usable, local_cols, rows_total).reshape(-1)
    row_flat = jnp.broadcast_to(own_slots[:, None], (grid_z, 7)).reshape(-1)
    empty_grid = jnp.zeros((grid_z, vectors, rows_total, vectors), jnp.float32)
    gathered = empty_grid.at[row_flat, :, col_flat, :].add(
        lax.all_gather(owned, "gz", axis=0, tiled=True), mode="drop"
    )
    coarse = gathered.reshape(grid_z * vectors, rows_total * vectors)
    rows_local = coarse.shape[0]
    cols_local = coarse.shape[1]
    panel_width = min(PANEL, rows_local, cols_local)
    global_rows = row_index * rows_local + jnp.arange(rows_local, dtype=jnp.int32)
    global_cols = index_z * cols_local + jnp.arange(cols_local, dtype=jnp.int32)
    offsets = jnp.arange(panel_width, dtype=jnp.int32)
    for panel_index in range(NPAN):
        panel_begin = panel_index * panel_width
        panel_end = panel_begin + panel_width
        row_root = panel_begin // rows_local
        col_root = panel_begin // cols_local
        row_start = panel_begin - row_root * rows_local
        col_start = panel_begin - col_root * cols_local
        column_piece = from_root(coarse[:, col_start : col_start + panel_width], "gz", col_root)
        row_piece, diagonal_piece = (
            from_root(coarse[row_start : row_start + panel_width, :], ("gx", "gy"), row_root),
            from_root(column_piece[row_start : row_start + panel_width, :], ("gx", "gy"), row_root),
        )
        factor = jnp.linalg.cholesky(diagonal_piece)
        row_factor = jax.scipy.linalg.solve_triangular(factor, column_piece.T, lower=True).T
        col_factor = jax.scipy.linalg.solve_triangular(factor, row_piece, lower=True).T
        row_factor = jnp.where(
            global_rows[:, None] >= panel_begin + offsets[None, :], row_factor, 0.0
        )
        updated = coarse - jnp.dot(row_factor, col_factor.T, precision=highest)
        trail_rows = global_rows >= panel_end
        trail_cols = global_cols >= panel_end
        panel_rows = (global_rows >= panel_begin) & (global_rows < panel_end)
        coarse = jnp.where(
            trail_rows[:, None] & trail_cols[None, :],
            updated,
            jnp.where(panel_rows[:, None] & trail_cols[None, :], 0.0, coarse),
        )
        old_columns = coarse[:, col_start : col_start + panel_width]
        new_columns = jnp.where(index_z == col_root, row_factor, old_columns)
        coarse = coarse.at[:, col_start : col_start + panel_width].set(new_columns)
    return coarse


def solution(mesh):
    in_specs = (P(None, "gx", "gy", "gz"), P("gx", "gy", "gz"), P(), P())
    out_specs = P(("gx", "gy"), "gz")
    return jax.shard_map(
        on_device, mesh=mesh, in_specs=in_specs, out_specs=out_specs, check_vma=False
    )
```

profile of v0, /device:TPU:1, one launch (start us, length us, event | category | flops | bytes accessed | tf_op | source)
XLA Modules:
  0.0 1363.8 jit_solution(13902177501467770364)
XLA Ops:
  23.9 15.8 %collective-permute-start.3 = (f32[4,1,128]{2,1,0:T(1,128)S(1)}, f32[4,1,128]{2,1,0:T(1,128)S(1)}, u32[]{:S(2)}, u32[]{:S(2)}) collective-permute-start(f32[4,1,128]{2,1,0:T(1,128)S(1)} %get-tuple-element.143), channel_id=1, source_target_pairs={{0,16},{16,32},{32,48},{1,17},{17,33},{33,49},{2,18},{18,34},{34,5... | collective-permute-start | bytes 6152 | tf_op jit(solution)/shard_map/ppermute | solution.py:20
  41.7 11.6 collective-permute-done.2
  62.7 12.4 collective-permute-start.9
  94.5 14.7 %collective-permute-start.15 = (f32[32,4,1,128]{3,0,2,1:T(8,128)S(1)}, f32[32,4,1,128]{3,0,2,1:T(8,128)S(1)}, u32[]{:S(2)}, u32[]{:S(2)}) collective-permute-start(f32[32,4,1,128]{3,0,2,1:T(8,128)S(1)} %get-tuple-element.117), channel_id=1, source_target_pairs={{0,16},{16,32},{32,48},{1,17},{17,33},{33,49},{2,18},{18,34},{34,5... | collective-permute-start | bytes 196616 | tf_op jit(solution)/shard_map/ppermute | solution.py:20
  130.0 14.2 %collective-permute-start.21 = (f32[32,4,1,128]{3,0,2,1:T(8,128)S(1)}, f32[32,4,1,128]{3,0,2,1:T(8,128)S(1)}, u32[]{:S(2)}, u32[]{:S(2)}) collective-permute-start(f32[32,4,1,128]{3,0,2,1:T(8,128)S(1)} %get-tuple-element.115), channel_id=1, source_target_pairs={{0,16},{16,32},{32,48},{1,17},{17,33},{33,49},{2,18},{18,34},{34,5... | collective-permute-start | bytes 196616 | tf_op jit(solution)/shard_map/ppermute | solution.py:20
  163.8 15.1 %collective-permute-start.27 = (f32[32,4,1,128]{3,0,2,1:T(8,128)S(1)}, f32[32,4,1,128]{3,0,2,1:T(8,128)S(1)}, u32[]{:S(2)}, u32[]{:S(2)}) collective-permute-start(f32[32,4,1,128]{3,0,2,1:T(8,128)S(1)} %get-tuple-element.113), channel_id=1, source_target_pairs={{0,16},{16,32},{32,48},{1,17},{17,33},{33,49},{2,18},{18,34},{34,5... | collective-permute-start | bytes 196616 | tf_op jit(solution)/shard_map/ppermute | solution.py:20
  203.7 15.1 %collective-permute-start.32 = (f32[32,4,1,128]{3,0,2,1:T(8,128)S(1)}, f32[32,4,1,128]{3,0,2,1:T(8,128)S(1)}, u32[]{:S(2)}, u32[]{:S(2)}) collective-permute-start(f32[32,4,1,128]{3,0,2,1:T(8,128)S(1)} %get-tuple-element.112), channel_id=1, source_target_pairs={{0,16},{16,32},{32,48},{1,17},{17,33},{33,49},{2,18},{18,34},{34,5... | collective-permute-start | bytes 196616 | tf_op jit(solution)/shard_map/ppermute | solution.py:20
  221.5 12.0 collective-permute-done.33
  247.8 212.4 %all-gather = f32[224,32,32]{2,1,0:T(8,128)S(1)} all-gather(f32[7,32,32]{2,1,0:T(8,128)S(1)} %fusion.2), channel_id=2, replica_groups=mesh['gx'=8,'gy'=4,'gz'=16] {'gx','gy'}, dimensions={0}, use_global_device_ids=true | all-gather | bytes 946176 | tf_op jit(solution)/shard_map/all_gather | solution.py:146
  460.7 50.5 %all_gather.7 = f32[112,32,32]{2,1,0:T(8,128)S(1)} all-gather(f32[7,32,32]{2,1,0:T(8,128)S(1)} %select_reduce_fusion), channel_id=1, replica_groups=mesh['gx'=8,'gy'=4,'gz'=16] {'gz'}, dimensions={0}, use_global_device_ids=true | all-gather | bytes 487424 | tf_op jit(solution)/shard_map/all_gather | solution.py:190
  515.5 16.4 %scatter_fusion = f32[16,32,32,32]{3,1,2,0:T(8,128)} fusion(f32[16,32,32,32]{3,1,2,0:T(8,128)} %broadcast_in_dim.82, s32[112]{0:T(128)S(1)} %fusion.191, f32[112,32,32]{2,1,0:T(8,128)S(1)} %all_gather.7), kind=kCustom, calls=%fused_computation | custom fusion | flops 114688 | bytes 1377152 | tf_op jit(solution)/shard_map/scatter-add | solution.py:189
  531.9 9.0 copy.208
  560.1 101.7 %all-reduce.9.cloned.1.call-done = f32[512,256]{0,1:T(8,128)} async-done(((f32[512,256]{0,1:T(8,128)}), f32[512,256]{0,1:T(8,128)}) %all-reduce.9.cloned.1.call-update) | async-done | bytes 524304 | tf_op jit(solution)/shard_map/psum | solution.py:30
  664.6 214.9 %all-reduce.15.cloned.1.call-done = (f32[256,1024]{1,0:T(8,128)}, f32[256,256]{0,1:T(8,128)}) async-done(((f32[256,1024]{1,0:T(8,128)}, f32[256,256]{0,1:T(8,128)}), (f32[256,1024]{1,0:T(8,128)}, f32[256,256]{0,1:T(8,128)})) %all-reduce.15.cloned.1.call-update) | async-done | bytes 1310736 | tf_op jit(solution)/shard_map/psum | solution.py:30
  881.6 11.7 cholesky.130
  893.3 9.8 custom-call.19
  903.6 11.7 cholesky.147
  922.2 19.8 %custom-call.20 = f32[2,128,128]{1,2,0:T(8,128)S(1)} custom-call(f32[2,128,128]{2,1,0:T(8,128)S(1)} %get-tuple-element.60), custom_call_target="InvertDiagBlocksLowerTriangular" | custom-call | tf_op jit(solution)/shard_map/jit(_solve_triangular)/triangular_solve | solution.py:212
  950.6 113.2 %all-reduce.11.cloned.1.call-done = f32[512,256]{0,1:T(8,128)} async-done(((f32[512,256]{0,1:T(8,128)}), f32[512,256]{0,1:T(8,128)}) %all-reduce.11.cloned.1.call-update) | async-done | bytes 524304 | tf_op jit(solution)/shard_map/psum | solution.py:30
  1066.4 214.9 %all-reduce.13.cloned.1.call-done = (f32[256,1024]{0,1:T(8,128)}, f32[256,256]{0,1:T(8,128)}) async-done(((f32[256,1024]{0,1:T(8,128)}, f32[256,256]{0,1:T(8,128)}), (f32[256,1024]{0,1:T(8,128)}, f32[256,256]{0,1:T(8,128)})) %all-reduce.13.cloned.1.call-update) | async-done | bytes 1310736 | tf_op jit(solution)/shard_map/psum | solution.py:30
  1283.5 11.7 cholesky.164
  1295.2 9.8 custom-call.22
  1305.5 11.7 cholesky.181
  1323.9 19.9 %custom-call.23 = f32[2,128,128]{1,2,0:T(8,128)S(1)} custom-call(f32[2,128,128]{2,1,0:T(8,128)S(1)} %get-tuple-element.62), custom_call_target="InvertDiagBlocksLowerTriangular" | custom-call | tf_op jit(solution)/shard_map/jit(_solve_triangular)/triangular_solve | solution.py:212
  (264 shorter events, 204.3 us)
Async XLA Ops:
  6.5 655.2 %all-reduce.9.cloned.1.call-start = ((), (), s32[]{:S(2)}) async-start(), calls=%async_computation | async-start | bytes 1048576 | tf_op jit(solution)/shard_map/psum | solution.py:30
  7.3 16.5 %collective-permute-start = (f32[1,8,128]{2,1,0:T(8,128)S(1)}, f32[1,8,128]{2,1,0:T(8,128)S(1)}, u32[]{:S(2)}, u32[]{:S(2)}) collective-permute-start(f32[1,8,128]{2,1,0:T(8,128)S(1)} %get-tuple-element.146), channel_id=1, source_target_pairs={{64,0},{128,64},{192,128},{256,192},{320,256},{384,320},{448,384},... | collective-permute-start | bytes 12296 | tf_op jit(solution)/shard_map/ppermute | solution.py:23
  8.7 15.2 %collective-permute-start.1 = (f32[1,8,128]{2,1,0:T(8,128)S(1)}, f32[1,8,128]{2,1,0:T(8,128)S(1)}, u32[]{:S(2)}, u32[]{:S(2)}) collective-permute-start(f32[1,8,128]{2,1,0:T(8,128)S(1)} %get-tuple-element.145), channel_id=1, source_target_pairs={{0,64},{64,128},{128,192},{192,256},{256,320},{320,384},{384,448},... | collective-permute-start | bytes 12296 | tf_op jit(solution)/shard_map/ppermute | solution.py:20
  14.7 45.0 %collective-permute-start.7 = (f32[32,1,8,128]{3,0,2,1:T(8,128)S(1)}, f32[32,1,8,128]{3,0,2,1:T(8,128)S(1)}, u32[]{:S(2)}, u32[]{:S(2)}) collective-permute-start(f32[32,1,8,128]{3,0,2,1:T(8,128)S(1)} %get-tuple-element.130), channel_id=1, source_target_pairs={{0,64},{64,128},{128,192},{192,256},{256,320},{320,384},{384,448},... | collective-permute-start | bytes 393224 | tf_op jit(solution)/shard_map/ppermute | solution.py:20
  18.3 42.5 %collective-permute-start.6 = (f32[32,1,8,128]{3,0,2,1:T(8,128)S(1)}, f32[32,1,8,128]{3,0,2,1:T(8,128)S(1)}, u32[]{:S(2)}, u32[]{:S(2)}) collective-permute-start(f32[32,1,8,128]{3,0,2,1:T(8,128)S(1)} %get-tuple-element.129), channel_id=1, source_target_pairs={{64,0},{128,64},{192,128},{256,192},{320,256},{384,320},{448,384},... | collective-permute-start | bytes 393224 | tf_op jit(solution)/shard_map/ppermute | solution.py:23
  23.9 17.7 %collective-permute-start.3 = (f32[4,1,128]{2,1,0:T(1,128)S(1)}, f32[4,1,128]{2,1,0:T(1,128)S(1)}, u32[]{:S(2)}, u32[]{:S(2)}) collective-permute-start(f32[4,1,128]{2,1,0:T(1,128)S(1)} %get-tuple-element.143), channel_id=1, source_target_pairs={{0,16},{16,32},{32,48},{1,17},{17,33},{33,49},{2,18},{18,34},{34,5... | collective-permute-start | bytes 6152 | tf_op jit(solution)/shard_map/ppermute | solution.py:20
  39.7 13.6 collective-permute-start.2
  60.8 14.4 %collective-permute-start.8 = (f32[32,4,1,128]{3,0,2,1:T(8,128)S(1)}, f32[32,4,1,128]{3,0,2,1:T(8,128)S(1)}, u32[]{:S(2)}, u32[]{:S(2)}) collective-permute-start(f32[32,4,1,128]{3,0,2,1:T(8,128)S(1)} %get-tuple-element.120), channel_id=1, source_target_pairs={{16,0},{32,16},{48,32},{17,1},{33,17},{49,33},{18,2},{34,18},{50,3... | collective-permute-start | bytes 196616 | tf_op jit(solution)/shard_map/ppermute | solution.py:23
  62.7 13.8 %collective-permute-start.9 = (f32[32,4,1,128]{3,0,2,1:T(8,128)S(1)}, f32[32,4,1,128]{3,0,2,1:T(8,128)S(1)}, u32[]{:S(2)}, u32[]{:S(2)}) collective-permute-start(f32[32,4,1,128]{3,0,2,1:T(8,128)S(1)} %get-tuple-element.119), channel_id=1, source_target_pairs={{0,16},{16,32},{32,48},{1,17},{17,33},{33,49},{2,18},{18,34},{34,5... | collective-permute-start | bytes 196616 | tf_op jit(solution)/shard_map/ppermute | solution.py:20
  92.6 16.8 %collective-permute-start.14 = (f32[32,4,1,128]{3,0,2,1:T(8,128)S(1)}, f32[32,4,1,128]{3,0,2,1:T(8,128)S(1)}, u32[]{:S(2)}, u32[]{:S(2)}) collective-permute-start(f32[32,4,1,128]{3,0,2,1:T(8,128)S(1)} %get-tuple-element.118), channel_id=1, source_target_pairs={{16,0},{32,16},{48,32},{17,1},{33,17},{49,33},{18,2},{34,18},{50,3... | collective-permute-start | bytes 196616 | tf_op jit(solution)/shard_map/ppermute | solution.py:23
  94.5 16.3 %collective-permute-start.15 = (f32[32,4,1,128]{3,0,2,1:T(8,128)S(1)}, f32[32,4,1,128]{3,0,2,1:T(8,128)S(1)}, u32[]{:S(2)}, u32[]{:S(2)}) collective-permute-start(f32[32,4,1,128]{3,0,2,1:T(8,128)S(1)} %get-tuple-element.117), channel_id=1, source_target_pairs={{0,16},{16,32},{32,48},{1,17},{17,33},{33,49},{2,18},{18,34},{34,5... | collective-permute-start | bytes 196616 | tf_op jit(solution)/shard_map/ppermute | solution.py:20
  111.5 7.3 collective-permute-start.16
  128.1 16.8 %collective-permute-start.20 = (f32[32,4,1,128]{3,0,2,1:T(8,128)S(1)}, f32[32,4,1,128]{3,0,2,1:T(8,128)S(1)}, u32[]{:S(2)}, u32[]{:S(2)}) collective-permute-start(f32[32,4,1,128]{3,0,2,1:T(8,128)S(1)} %get-tuple-element.116), channel_id=1, source_target_pairs={{16,0},{32,16},{48,32},{17,1},{33,17},{49,33},{18,2},{34,18},{50,3... | collective-permute-start | bytes 196616 | tf_op jit(solution)/shard_map/ppermute | solution.py:23
  130.0 15.6 %collective-permute-start.21 = (f32[32,4,1,128]{3,0,2,1:T(8,128)S(1)}, f32[32,4,1,128]{3,0,2,1:T(8,128)S(1)}, u32[]{:S(2)}, u32[]{:S(2)}) collective-permute-start(f32[32,4,1,128]{3,0,2,1:T(8,128)S(1)} %get-tuple-element.115), channel_id=1, source_target_pairs={{0,16},{16,32},{32,48},{1,17},{17,33},{33,49},{2,18},{18,34},{34,5... | collective-permute-start | bytes 196616 | tf_op jit(solution)/shard_map/ppermute | solution.py:20
  161.9 17.2 %collective-permute-start.26 = (f32[32,4,1,128]{3,0,2,1:T(8,128)S(1)}, f32[32,4,1,128]{3,0,2,1:T(8,128)S(1)}, u32[]{:S(2)}, u32[]{:S(2)}) collective-permute-start(f32[32,4,1,128]{3,0,2,1:T(8,128)S(1)} %get-tuple-element.114), channel_id=1, source_target_pairs={{16,0},{32,16},{48,32},{17,1},{33,17},{49,33},{18,2},{34,18},{50,3... | collective-permute-start | bytes 196616 | tf_op jit(solution)/shard_map/ppermute | solution.py:23
  163.8 16.4 %collective-permute-start.27 = (f32[32,4,1,128]{3,0,2,1:T(8,128)S(1)}, f32[32,4,1,128]{3,0,2,1:T(8,128)S(1)}, u32[]{:S(2)}, u32[]{:S(2)}) collective-permute-start(f32[32,4,1,128]{3,0,2,1:T(8,128)S(1)} %get-tuple-element.113), channel_id=1, source_target_pairs={{0,16},{16,32},{32,48},{1,17},{17,33},{33,49},{2,18},{18,34},{34,5... | collective-permute-start | bytes 196616 | tf_op jit(solution)/shard_map/ppermute | solution.py:20
  189.0 8.7 collective-permute-start.30
  195.5 8.2 collective-permute-start.31
  203.7 17.8 %collective-permute-start.32 = (f32[32,4,1,128]{3,0,2,1:T(8,128)S(1)}, f32[32,4,1,128]{3,0,2,1:T(8,128)S(1)}, u32[]{:S(2)}, u32[]{:S(2)}) collective-permute-start(f32[32,4,1,128]{3,0,2,1:T(8,128)S(1)} %get-tuple-element.112), channel_id=1, source_target_pairs={{0,16},{16,32},{32,48},{1,17},{17,33},{33,49},{2,18},{18,34},{34,5... | collective-permute-start | bytes 196616 | tf_op jit(solution)/shard_map/ppermute | solution.py:20
  218.8 14.7 %collective-permute-start.33 = (f32[32,4,1,128]{3,0,2,1:T(8,128)S(1)}, f32[32,4,1,128]{3,0,2,1:T(8,128)S(1)}, u32[]{:S(2)}, u32[]{:S(2)}) collective-permute-start(f32[32,4,1,128]{3,0,2,1:T(8,128)S(1)} %get-tuple-element.111), channel_id=1, source_target_pairs={{16,0},{32,16},{48,32},{17,1},{33,17},{49,33},{18,2},{34,18},{50,3... | collective-permute-start | bytes 196616 | tf_op jit(solution)/shard_map/ppermute | solution.py:23
  234.1 8.0 collective-permute-start.34
  548.1 331.4 %all-reduce.15.cloned.1.call-start = ((), (), s32[]{:S(2)}) async-start(), calls=%async_computation.3 | async-start | bytes 2621440 | tf_op jit(solution)/shard_map/psum | solution.py:30
  663.5 400.4 %all-reduce.11.cloned.1.call-start = ((), (), s32[]{:S(2)}) async-start(), calls=%async_computation.1 | async-start | bytes 1048576 | tf_op jit(solution)/shard_map/psum | solution.py:30
  949.5 331.9 %all-reduce.13.cloned.1.call-start = ((), (), s32[]{:S(2)}) async-start(), calls=%async_computation.2 | async-start | bytes 2621440 | tf_op jit(solution)/shard_map/psum | solution.py:30
  (24 other events, 719.3 us)
Sparse Core Ops, SparseCore 0:
  548.2 113.5 all-reduce.8
  664.2 215.2 all-reduce.14
  949.6 114.1 all-reduce.10
  1066.1 215.2 all-reduce.12
where the time goes:
time: 1370 us; the launch traced here: 1360 us
  waiting for transfers between devices  692 us (51%)
  blocking collectives  263 us (19%)
  starting transfers between devices  173 us (13%)
  other arithmetic  151 us (11%)
  local copies, waits for them, and re-layouts  51.9 us (4%)
  between operations  17.3 us (1%)
  matrix products  15.8 us (1%)
    psum x4, waiting for transfers between devices, from_root(): return lax.psum(kept, axis)  645 us
    all_gather x1, blocking collectives, on_device(): piece = lax.all_gather(blocks[None], ('gx', 'gy'), axis=0, tiled=True)  212 us
    ppermute x18, starting transfers between devices, with_halo(): lax.ppermute(lax.slice_in_dim(block, block.shape[dim] - width, None, axis...  145 us
    another operation x14, other arithmetic, on_device(): factor = jnp.linalg.cholesky(diagonal_piece)  69.3 us
    all_gather x1, blocking collectives, on_device(): lax.all_gather(owned, 'gz', axis=0, tiled=True)  50.5 us
    another operation x5, other arithmetic, on_device(): jax.scipy.linalg.solve_triangular(factor, column_piece.T, lower=True)  39.8 us
    ppermute x18, waiting for transfers between devices, with_halo(): lax.ppermute(lax.slice_in_dim(block, 0, width, axis=dim), axis, backward)  36 us
  transfers between devices with their start and end apart: 40, of which 24 were waited for; matrix products, arithmetic and copies ran while one was open for 2% of the time, Pallas kernels for 0%

commit v1 on v0

--- a/solution.py
+++ b/solution.py
@@ -143,7 +143,10 @@
     group_of = slot_order // grid_z
     column_groups = lax.dynamic_index_in_dim(group_of, index_z, 1, keepdims=False)
     owner_source = jnp.sum(jnp.where(column_groups == row_index, row_ids, 0))
-    piece = lax.all_gather(blocks[None], ("gx", "gy"), axis=0, tiled=True)
+    piece = jnp.concatenate(
+        lax.all_to_all(jnp.stack([blocks[None]] * lax.axis_size(("gx", "gy"))), ("gx", "gy"), 0, 0),
+        axis=0,
+    )
     anchor = jnp.arange(piece.shape[0], dtype=jnp.int32)
     wanted = (anchor == owner_source)[:, None, None, None]
     owned = jnp.sum(jnp.where(wanted, piece, 0.0), axis=0)

time: 1370 us -> 1210 us (0.88)
  blocking collectives: 263 us -> 30.6 us
  waiting for transfers between devices: 692 us -> 731 us
    all_gather x1 -> x0, blocking collectives: 212 us -> none  [on_device(): piece = lax.all_gather(blocks[None], ('gx', 'gy'), axis=0, tiled=True)]
    all_to_all x0 -> x1, waiting for transfers between devices: none -> 37.4 us  [on_device(): lax.all_to_all(jnp.stack([blocks[None]] * lax.axis_size(('gx', 'gy'))), (...]
    all_gather x1, blocking collectives: 50.5 us -> 30.6 us  [on_device(): lax.all_gather(owned, 'gz', axis=0, tiled=True)]
  transfers between devices with their start and end apart: 40 -> 41, of which waited for: 24 -> 27; matrix products, arithmetic and copies ran while one was open for 2% -> 2% of each run, Pallas kernels for 0% -> 0%
where the time goes in v1:
time: 1210 us; the launch traced here: 1190 us
  waiting for transfers between devices  731 us (60%)
  starting transfers between devices  183 us (15%)
  other arithmetic  154 us (13%)
  local copies, waits for them, and re-layouts  61.5 us (5%)
  blocking collectives  30.6 us (3%)
  between operations  17.4 us (1%)
  matrix products  15.8 us (1%)
    psum x4, waiting for transfers between devices, from_root(): return lax.psum(kept, axis)  646 us
    ppermute x18, starting transfers between devices, with_halo(): lax.ppermute(lax.slice_in_dim(block, block.shape[dim] - width, None, axis...  144 us
    another operation x14, other arithmetic, on_device(): factor = jnp.linalg.cholesky(diagonal_piece)  69.3 us
    another operation x5, other arithmetic, on_device(): jax.scipy.linalg.solve_triangular(factor, column_piece.T, lower=True)  39.8 us
    all_to_all x1, waiting for transfers between devices, on_device(): lax.all_to_all(jnp.stack([blocks[None]] * lax.axis_size(('gx', 'gy'))), (...  37.4 us
    ppermute x18, waiting for transfers between devices, with_halo(): lax.ppermute(lax.slice_in_dim(block, 0, width, axis=dim), axis, backward)  36.8 us
    all_gather x1, blocking collectives, on_device(): lax.all_gather(owned, 'gz', axis=0, tiled=True)  30.6 us
    ppermute x18, starting transfers between devices, with_halo(): lax.ppermute(lax.slice_in_dim(block, 0, width, axis=dim), axis, backward)  27 us
  transfers between devices with their start and end apart: 41, of which 27 were waited for; matrix products, arithmetic and copies ran while one was open for 2% of the time, Pallas kernels for 0%

profile of v1, /device:TPU:1, one launch (start us, length us, event | category | flops | bytes accessed | tf_op | source)
XLA Modules:
  0.0 1194.5 jit_solution(10513248559507528089)
XLA Ops:
  14.7 16.6 %collective-permute-start.3 = (f32[4,1,128]{2,1,0:T(1,128)S(1)}, f32[4,1,128]{2,1,0:T(1,128)S(1)}, u32[]{:S(2)}, u32[]{:S(2)}) collective-permute-start(f32[4,1,128]{2,1,0:T(1,128)S(1)} %get-tuple-element.143), channel_id=1, source_target_pairs={{0,16},{16,32},{32,48},{1,17},{17,33},{33,49},{2,18},{18,34},{34,5... | collective-permute-start | bytes 6152 | tf_op jit(solution)/shard_map/ppermute | solution.py:20
  58.6 12.4 %collective-permute-start.9 = (f32[32,4,1,128]{3,0,2,1:T(8,128)S(1)}, f32[32,4,1,128]{3,0,2,1:T(8,128)S(1)}, u32[]{:S(2)}, u32[]{:S(2)}) collective-permute-start(f32[32,4,1,128]{3,0,2,1:T(8,128)S(1)} %get-tuple-element.119), channel_id=1, source_target_pairs={{0,16},{16,32},{32,48},{1,17},{17,33},{33,49},{2,18},{18,34},{34,5... | collective-permute-start | bytes 196616 | tf_op jit(solution)/shard_map/ppermute | solution.py:20
  89.2 15.6 %collective-permute-start.15 = (f32[32,4,1,128]{3,0,2,1:T(8,128)S(1)}, f32[32,4,1,128]{3,0,2,1:T(8,128)S(1)}, u32[]{:S(2)}, u32[]{:S(2)}) collective-permute-start(f32[32,4,1,128]{3,0,2,1:T(8,128)S(1)} %get-tuple-element.117), channel_id=1, source_target_pairs={{0,16},{16,32},{32,48},{1,17},{17,33},{33,49},{2,18},{18,34},{34,5... | collective-permute-start | bytes 196616 | tf_op jit(solution)/shard_map/ppermute | solution.py:20
  124.4 14.8 %collective-permute-start.21 = (f32[32,4,1,128]{3,0,2,1:T(8,128)S(1)}, f32[32,4,1,128]{3,0,2,1:T(8,128)S(1)}, u32[]{:S(2)}, u32[]{:S(2)}) collective-permute-start(f32[32,4,1,128]{3,0,2,1:T(8,128)S(1)} %get-tuple-element.115), channel_id=1, source_target_pairs={{0,16},{16,32},{32,48},{1,17},{17,33},{33,49},{2,18},{18,34},{34,5... | collective-permute-start | bytes 196616 | tf_op jit(solution)/shard_map/ppermute | solution.py:20
  158.8 15.0 %collective-permute-start.27 = (f32[32,4,1,128]{3,0,2,1:T(8,128)S(1)}, f32[32,4,1,128]{3,0,2,1:T(8,128)S(1)}, u32[]{:S(2)}, u32[]{:S(2)}) collective-permute-start(f32[32,4,1,128]{3,0,2,1:T(8,128)S(1)} %get-tuple-element.113), channel_id=1, source_target_pairs={{0,16},{16,32},{32,48},{1,17},{17,33},{33,49},{2,18},{18,34},{34,5... | collective-permute-start | bytes 196616 | tf_op jit(solution)/shard_map/ppermute | solution.py:20
  197.2 16.1 %collective-permute-start.32 = (f32[32,4,1,128]{3,0,2,1:T(8,128)S(1)}, f32[32,4,1,128]{3,0,2,1:T(8,128)S(1)}, u32[]{:S(2)}, u32[]{:S(2)}) collective-permute-start(f32[32,4,1,128]{3,0,2,1:T(8,128)S(1)} %get-tuple-element.112), channel_id=1, source_target_pairs={{0,16},{16,32},{32,48},{1,17},{17,33},{33,49},{2,18},{18,34},{34,5... | collective-permute-start | bytes 196616 | tf_op jit(solution)/shard_map/ppermute | solution.py:20
  215.8 13.0 %collective-permute-done.33 = f32[32,4,1,128]{3,0,2,1:T(8,128)S(1)} collective-permute-done((f32[32,4,1,128]{3,0,2,1:T(8,128)S(1)}, f32[32,4,1,128]{3,0,2,1:T(8,128)S(1)}, u32[]{:S(2)}, u32[]{:S(2)}) %collective-permute-start.33) | collective-permute-done | bytes 65568 | tf_op jit(solution)/shard_map/ppermute | solution.py:23
  247.1 11.6 all-to-all-start
  264.2 37.4 %all-to-all-done = f32[32,1,7168]{2,1,0:T(1,128)S(1)} async-done(((f32[32,1,7168]{2,1,0:T(1,128)}), f32[32,1,7168]{2,1,0:T(1,128)S(1)}, u32[]{:S(2)}, u32[]{:S(2)}) %all-to-all-start) | async-done | bytes 917536 | tf_op jit(solution)/shard_map/all_to_all | solution.py:147
  310.0 30.6 %all_gather.3 = f32[112,32,32]{2,1,0:T(8,128)S(1)} all-gather(f32[7,32,32]{2,1,0:T(8,128)S(1)} %fusion), channel_id=1, replica_groups=mesh['gx'=8,'gy'=4,'gz'=16] {'gz'}, dimensions={0}, use_global_device_ids=true | all-gather | bytes 487424 | tf_op jit(solution)/shard_map/all_gather | solution.py:193
  345.0 16.4 %scatter_fusion = f32[16,32,32,32]{3,1,2,0:T(8,128)} fusion(f32[16,32,32,32]{3,1,2,0:T(8,128)} %broadcast_in_dim.79, s32[112]{0:T(128)S(1)} %fusion.192, f32[112,32,32]{2,1,0:T(8,128)S(1)} %all_gather.3), kind=kCustom, calls=%fused_computation | custom fusion | flops 114688 | bytes 1377152 | tf_op jit(solution)/shard_map/scatter-add | solution.py:192
  361.4 9.0 copy.208
  389.6 102.7 %all-reduce.9.cloned.1.call-done = f32[512,256]{0,1:T(8,128)} async-done(((f32[512,256]{0,1:T(8,128)}), f32[512,256]{0,1:T(8,128)}) %all-reduce.9.cloned.1.call-update) | async-done | bytes 524304 | tf_op jit(solution)/shard_map/psum | solution.py:30
  495.1 214.8 %all-reduce.15.cloned.1.call-done = (f32[256,1024]{1,0:T(8,128)}, f32[256,256]{0,1:T(8,128)}) async-done(((f32[256,1024]{1,0:T(8,128)}, f32[256,256]{0,1:T(8,128)}), (f32[256,1024]{1,0:T(8,128)}, f32[256,256]{0,1:T(8,128)})) %all-reduce.15.cloned.1.call-update) | async-done | bytes 1310736 | tf_op jit(solution)/shard_map/psum | solution.py:30
  712.0 11.7 cholesky.130
  723.8 9.8 custom-call.19
  734.1 11.7 cholesky.147
  752.8 19.8 %custom-call.20 = f32[2,128,128]{1,2,0:T(8,128)S(1)} custom-call(f32[2,128,128]{2,1,0:T(8,128)S(1)} %get-tuple-element.60), custom_call_target="InvertDiagBlocksLowerTriangular" | custom-call | tf_op jit(solution)/shard_map/jit(_solve_triangular)/triangular_solve | solution.py:215
  781.3 113.2 %all-reduce.11.cloned.1.call-done = f32[512,256]{0,1:T(8,128)} async-done(((f32[512,256]{0,1:T(8,128)}), f32[512,256]{0,1:T(8,128)}) %all-reduce.11.cloned.1.call-update) | async-done | bytes 524304 | tf_op jit(solution)/shard_map/psum | solution.py:30
  897.1 215.0 %all-reduce.13.cloned.1.call-done = (f32[256,1024]{0,1:T(8,128)}, f32[256,256]{0,1:T(8,128)}) async-done(((f32[256,1024]{0,1:T(8,128)}, f32[256,256]{0,1:T(8,128)}), (f32[256,1024]{0,1:T(8,128)}, f32[256,256]{0,1:T(8,128)})) %all-reduce.13.cloned.1.call-update) | async-done | bytes 1310736 | tf_op jit(solution)/shard_map/psum | solution.py:30
  1114.1 11.7 cholesky.164
  1125.9 9.8 custom-call.22
  1136.2 11.7 cholesky.181
  1154.6 19.9 %custom-call.23 = f32[2,128,128]{1,2,0:T(8,128)S(1)} custom-call(f32[2,128,128]{2,1,0:T(8,128)S(1)} %get-tuple-element.62), custom_call_target="InvertDiagBlocksLowerTriangular" | custom-call | tf_op jit(solution)/shard_map/jit(_solve_triangular)/triangular_solve | solution.py:215
  (270 shorter events, 224.9 us)
Async XLA Ops:
  7.3 7.3 collective-permute-start
  14.7 22.5 %collective-permute-start.3 = (f32[4,1,128]{2,1,0:T(1,128)S(1)}, f32[4,1,128]{2,1,0:T(1,128)S(1)}, u32[]{:S(2)}, u32[]{:S(2)}) collective-permute-start(f32[4,1,128]{2,1,0:T(1,128)S(1)} %get-tuple-element.143), channel_id=1, source_target_pairs={{0,16},{16,32},{32,48},{1,17},{17,33},{33,49},{2,18},{18,34},{34,5... | collective-permute-start | bytes 6152 | tf_op jit(solution)/shard_map/ppermute | solution.py:20
  31.3 13.6 %collective-permute-start.2 = (f32[4,1,128]{2,1,0:T(1,128)S(1)}, f32[4,1,128]{2,1,0:T(1,128)S(1)}, u32[]{:S(2)}, u32[]{:S(2)}) collective-permute-start(f32[4,1,128]{2,1,0:T(1,128)S(1)} %get-tuple-element.144), channel_id=1, source_target_pairs={{16,0},{32,16},{48,32},{17,1},{33,17},{49,33},{18,2},{34,18},{50,3... | collective-permute-start | bytes 6152 | tf_op jit(solution)/shard_map/ppermute | solution.py:23
  33.3 18.5 %collective-permute-start.7 = (f32[32,1,8,128]{3,0,2,1:T(8,128)S(1)}, f32[32,1,8,128]{3,0,2,1:T(8,128)S(1)}, u32[]{:S(2)}, u32[]{:S(2)}) collective-permute-start(f32[32,1,8,128]{3,0,2,1:T(8,128)S(1)} %get-tuple-element.130), channel_id=1, source_target_pairs={{0,64},{64,128},{128,192},{192,256},{256,320},{320,384},{384,448},... | collective-permute-start | bytes 393224 | tf_op jit(solution)/shard_map/ppermute | solution.py:20
  56.6 14.5 %collective-permute-start.8 = (f32[32,4,1,128]{3,0,2,1:T(8,128)S(1)}, f32[32,4,1,128]{3,0,2,1:T(8,128)S(1)}, u32[]{:S(2)}, u32[]{:S(2)}) collective-permute-start(f32[32,4,1,128]{3,0,2,1:T(8,128)S(1)} %get-tuple-element.120), channel_id=1, source_target_pairs={{16,0},{32,16},{48,32},{17,1},{33,17},{49,33},{18,2},{34,18},{50,3... | collective-permute-start | bytes 196616 | tf_op jit(solution)/shard_map/ppermute | solution.py:23
  58.6 13.7 %collective-permute-start.9 = (f32[32,4,1,128]{3,0,2,1:T(8,128)S(1)}, f32[32,4,1,128]{3,0,2,1:T(8,128)S(1)}, u32[]{:S(2)}, u32[]{:S(2)}) collective-permute-start(f32[32,4,1,128]{3,0,2,1:T(8,128)S(1)} %get-tuple-element.119), channel_id=1, source_target_pairs={{0,16},{16,32},{32,48},{1,17},{17,33},{33,49},{2,18},{18,34},{34,5... | collective-permute-start | bytes 196616 | tf_op jit(solution)/shard_map/ppermute | solution.py:20
  87.3 17.5 %collective-permute-start.14 = (f32[32,4,1,128]{3,0,2,1:T(8,128)S(1)}, f32[32,4,1,128]{3,0,2,1:T(8,128)S(1)}, u32[]{:S(2)}, u32[]{:S(2)}) collective-permute-start(f32[32,4,1,128]{3,0,2,1:T(8,128)S(1)} %get-tuple-element.118), channel_id=1, source_target_pairs={{16,0},{32,16},{48,32},{17,1},{33,17},{49,33},{18,2},{34,18},{50,3... | collective-permute-start | bytes 196616 | tf_op jit(solution)/shard_map/ppermute | solution.py:23
  89.2 17.0 %collective-permute-start.15 = (f32[32,4,1,128]{3,0,2,1:T(8,128)S(1)}, f32[32,4,1,128]{3,0,2,1:T(8,128)S(1)}, u32[]{:S(2)}, u32[]{:S(2)}) collective-permute-start(f32[32,4,1,128]{3,0,2,1:T(8,128)S(1)} %get-tuple-element.117), channel_id=1, source_target_pairs={{0,16},{16,32},{32,48},{1,17},{17,33},{33,49},{2,18},{18,34},{34,5... | collective-permute-start | bytes 196616 | tf_op jit(solution)/shard_map/ppermute | solution.py:20
  122.5 16.9 %collective-permute-start.20 = (f32[32,4,1,128]{3,0,2,1:T(8,128)S(1)}, f32[32,4,1,128]{3,0,2,1:T(8,128)S(1)}, u32[]{:S(2)}, u32[]{:S(2)}) collective-permute-start(f32[32,4,1,128]{3,0,2,1:T(8,128)S(1)} %get-tuple-element.116), channel_id=1, source_target_pairs={{16,0},{32,16},{48,32},{17,1},{33,17},{49,33},{18,2},{34,18},{50,3... | collective-permute-start | bytes 196616 | tf_op jit(solution)/shard_map/ppermute | solution.py:23
  124.4 16.1 %collective-permute-start.21 = (f32[32,4,1,128]{3,0,2,1:T(8,128)S(1)}, f32[32,4,1,128]{3,0,2,1:T(8,128)S(1)}, u32[]{:S(2)}, u32[]{:S(2)}) collective-permute-start(f32[32,4,1,128]{3,0,2,1:T(8,128)S(1)} %get-tuple-element.115), channel_id=1, source_target_pairs={{0,16},{16,32},{32,48},{1,17},{17,33},{33,49},{2,18},{18,34},{34,5... | collective-permute-start | bytes 196616 | tf_op jit(solution)/shard_map/ppermute | solution.py:20
  150.2 6.6 collective-permute-start.25
  156.9 17.1 %collective-permute-start.26 = (f32[32,4,1,128]{3,0,2,1:T(8,128)S(1)}, f32[32,4,1,128]{3,0,2,1:T(8,128)S(1)}, u32[]{:S(2)}, u32[]{:S(2)}) collective-permute-start(f32[32,4,1,128]{3,0,2,1:T(8,128)S(1)} %get-tuple-element.114), channel_id=1, source_target_pairs={{16,0},{32,16},{48,32},{17,1},{33,17},{49,33},{18,2},{34,18},{50,3... | collective-permute-start | bytes 196616 | tf_op jit(solution)/shard_map/ppermute | solution.py:23
  158.8 16.3 %collective-permute-start.27 = (f32[32,4,1,128]{3,0,2,1:T(8,128)S(1)}, f32[32,4,1,128]{3,0,2,1:T(8,128)S(1)}, u32[]{:S(2)}, u32[]{:S(2)}) collective-permute-start(f32[32,4,1,128]{3,0,2,1:T(8,128)S(1)} %get-tuple-element.113), channel_id=1, source_target_pairs={{0,16},{16,32},{32,48},{1,17},{17,33},{33,49},{2,18},{18,34},{34,5... | collective-permute-start | bytes 196616 | tf_op jit(solution)/shard_map/ppermute | solution.py:20
  175.8 8.3 collective-permute-start.28
  177.4 7.4 collective-permute-start.29
  189.6 7.6 collective-permute-start.31
  197.2 18.5 %collective-permute-start.32 = (f32[32,4,1,128]{3,0,2,1:T(8,128)S(1)}, f32[32,4,1,128]{3,0,2,1:T(8,128)S(1)}, u32[]{:S(2)}, u32[]{:S(2)}) collective-permute-start(f32[32,4,1,128]{3,0,2,1:T(8,128)S(1)} %get-tuple-element.112), channel_id=1, source_target_pairs={{0,16},{16,32},{32,48},{1,17},{17,33},{33,49},{2,18},{18,34},{34,5... | collective-permute-start | bytes 196616 | tf_op jit(solution)/shard_map/ppermute | solution.py:20
  213.3 15.4 %collective-permute-start.33 = (f32[32,4,1,128]{3,0,2,1:T(8,128)S(1)}, f32[32,4,1,128]{3,0,2,1:T(8,128)S(1)}, u32[]{:S(2)}, u32[]{:S(2)}) collective-permute-start(f32[32,4,1,128]{3,0,2,1:T(8,128)S(1)} %get-tuple-element.111), channel_id=1, source_target_pairs={{16,0},{32,16},{48,32},{17,1},{33,17},{49,33},{18,2},{34,18},{50,3... | collective-permute-start | bytes 196616 | tf_op jit(solution)/shard_map/ppermute | solution.py:23
  233.2 7.2 collective-permute-start.35
  247.1 54.6 %all-to-all-start = ((f32[32,1,7168]{2,1,0:T(1,128)}), f32[32,1,7168]{2,1,0:T(1,128)S(1)}, u32[]{:S(2)}, u32[]{:S(2)}) async-start(f32[32,1,7168]{2,1,0:T(1,128)} %reshape.476), calls=%async_computation | async-start | bytes 1835008 | tf_op jit(solution)/shard_map/all_to_all | solution.py:147
  258.6 233.6 %all-reduce.9.cloned.1.call-start = ((), (), s32[]{:S(2)}) async-start(), calls=%async_computation.1 | async-start | bytes 1048576 | tf_op jit(solution)/shard_map/psum | solution.py:30
  377.6 332.4 %all-reduce.15.cloned.1.call-start = ((), (), s32[]{:S(2)}) async-start(), calls=%async_computation.4 | async-start | bytes 2621440 | tf_op jit(solution)/shard_map/psum | solution.py:30
  493.9 400.5 %all-reduce.11.cloned.1.call-start = ((), (), s32[]{:S(2)}) async-start(), calls=%async_computation.2 | async-start | bytes 1048576 | tf_op jit(solution)/shard_map/psum | solution.py:30
  780.1 331.9 %all-reduce.13.cloned.1.call-start = ((), (), s32[]{:S(2)}) async-start(), calls=%async_computation.3 | async-start | bytes 2621440 | tf_op jit(solution)/shard_map/psum | solution.py:30
  (25 other events, 729.8 us)
Sparse Core Ops, SparseCore 0:
  377.7 114.5 all-reduce.8
  494.6 215.2 all-reduce.14
  780.3 114.1 all-reduce.10
  896.7 215.2 all-reduce.12
